TPU v7x, 128 devices: a whole 4x4x4 slice. The times are simulated.
128 devices in a mesh: tensor: 8 (over z, core), fsdp: 16 (over x, y).
Axes of the slice: x: 4, y: 4, z: 4, core: 2. Of those that a mesh axis runs over, the one named last changes fastest.
Arguments:
- momentum: float32 [4096, 28672], P('tensor', 'fsdp'), may hold values from -6 to 6
- gradient: bfloat16 [4096, 28672], P('tensor', 'fsdp'), may hold values from -6 to 6
- right_factor: float32 [28672, 512], P('fsdp'), may hold values from -0.03125 to 0.03125
Outputs:
- new_momentum: float32 [4096, 28672], P('tensor', 'fsdp')
- update: float32 [4096, 28672], P('tensor', 'fsdp')
- new_right: float32 [28672, 512], P('fsdp')
All inputs are finite; a program needn't handle non-finite values.
Results may differ from a plain program's by a relative error of at most 0.0003.
Values sent between devices are 32-bit elements; how exact they have to be, the bound alone decides.
A program may use at most 128 MiB of HBM per device.

v0:
```python
import functools

import jax
import jax.numpy as jnp
from jax import lax
from jax.sharding import Mesh
from jax.sharding import PartitionSpec as P

ROWS = 4096
COLS = 28672
RANK = 512
FSDP = ("fsdp_0", "fsdp_1")
TENSOR = ("tensor_0", "tensor_1")
TENSOR_FSDP = ("tensor_0", "tensor_1", "fsdp_0", "fsdp_1")


def total_of_pieces(value, axis):
    parts = lax.all_gather(value, axis)
    return parts.sum(axis=0)


def in_blocks(value, dim, devices):
    lengths = value.shape
    parts = value.reshape(*lengths[:dim], devices, lengths[dim] // devices, *lengths[dim + 1 :])
    return jnp.moveaxis(parts, dim, 0)


def sum_at_owner(value, axis, dim):
    devices = lax.axis_size(axis)
    parts = lax.all_to_all(in_blocks(value, dim, devices), axis, 0, 0, tiled=True)
    return jnp.sum(parts, axis=0)


def over_axes(value, axes):
    return functools.reduce(lax.psum, axes, value)


def inner_rows(first, second):
    return lax.dot_general(
        first,
        second,
        (((0,), (0,)), ((), ())),
        precision=lax.Precision.HIGHEST,
        preferred_element_type=jnp.float32,
    )


def outer_rank(first, second):
    return lax.dot_general(
        first,
        second,
        (((1,), (1,)), ((), ())),
        precision=lax.Precision.HIGHEST,
        preferred_element_type=jnp.float32,
    )


def orthonormal(block, gram):
    lower = jnp.linalg.cholesky(gram)
    return jax.scipy.linalg.solve_triangular(lower, block.T, lower=True).T


def per_device(momentum, gradient, right_factor):
    buffer = momentum + gradient.astype(jnp.float32)
    partial_value = jnp.dot(
        buffer, right_factor, precision=lax.Precision.HIGHEST, preferred_element_type=jnp.float32
    )
    left = lax.psum(partial_value, FSDP)
    gram = total_of_pieces(inner_rows(left, left), TENSOR)
    ortho = orthonormal(left, gram)
    right_part = inner_rows(buffer, ortho)
    right_block = sum_at_owner(right_part, TENSOR, 0)
    colsq = over_axes(jnp.sum(right_block * right_block, axis=0), TENSOR_FSDP)
    right = lax.all_gather(right_block, TENSOR, axis=0, tiled=True)
    normed = right / jnp.sqrt(colsq + 1e-06)
    new_momentum = buffer - 0.05 * outer_rank(ortho, right)
    scale = jnp.sqrt(jnp.float32(ROWS * COLS / RANK))
    update = scale * outer_rank(ortho, normed)
    return (new_momentum, update, normed)


def solution(mesh):
    finer = Mesh(mesh.devices.reshape(4, 2, 4, 4), ("tensor_0", "tensor_1", "fsdp_0", "fsdp_1"))
    placed = (P(TENSOR, FSDP), P(TENSOR, FSDP), P(FSDP, None))
    return jax.shard_map(
        per_device,
        mesh=finer,
        in_specs=placed,
        out_specs=(P(TENSOR, FSDP), P(TENSOR, FSDP), P(FSDP, None)),
        check_vma=False,
    )
```

profile of v0, /device:TPU:1, one launch (start us, length us, event | category | flops | bytes accessed | tf_op | source)
XLA Modules:
  0.0 452.0 jit_solution(2981976357336586488)
XLA Ops:
  7.2 10.3 %fusion.1 = f32[512,512]{1,0:T(8,128)} fusion(f32[1792,512]{1,0:T(8,128)} %param.5, f32[512,1792]{1,0:T(8,128)} %param.3, bf16[512,1792]{1,0:T(8,128)(2,1)} %param.4), kind=kOutput, calls=%fused_computation.7 | convolution fusion | flops 5638979584 | bytes 10223616 | tf_op jit(solution)/shard_map/dot_general | solution.py:65
  17.6 88.9 %all-reduce.3.cloned.1.call-done = f32[512,512]{1,0:T(8,128)} async-done(((f32[512,512]{1,0:T(8,128)}), f32[512,512]{1,0:T(8,128)}) %all-reduce.3.cloned.1.call-update) | async-done | bytes 1048592 | tf_op jit(solution)/shard_map/psum | solution.py:68
  106.6 4.5 %fusion.36 = f32[512,512]{1,0:T(8,128)} fusion(f32[512,512]{1,0:T(8,128)} %all-reduce.3.cloned.1.call-done), kind=kOutput, calls=%fused_computation.78 | convolution fusion | flops 1610612736 | bytes 2097152 | tf_op jit(solution)/shard_map/dot_general | solution.py:39
  111.4 51.0 %all-gather.6.cloned.1.call-done = f32[4096,512]{1,0:T(8,128)} async-done(((f32[512,512]{1,0:T(8,128)}), f32[4096,512]{1,0:T(8,128)}) %all-gather.6.cloned.1.call-update) | async-done | bytes 8388624 | tf_op jit(solution)/shard_map/all_gather | solution.py:18
  162.3 4.5 reduce_sum.27
  168.4 11.7 %cholesky.104 = f32[128,128]{1,0:T(8,128)S(1)} custom-call(f32[128,128]{1,0:T(8,128)S(1)} %cholesky.266), custom_call_target="Cholesky" | custom-call | tf_op jit(solution)/shard_map/jit(cholesky)/cholesky | solution.py:59
  180.3 9.8 %custom-call.31 = f32[1,128,128]{1,2,0:T(8,128)S(1)} custom-call(f32[1,128,128]{2,1,0:T(8,128)S(1)} %get-tuple-element.30), custom_call_target="InvertDiagBlocksLowerTriangular" | custom-call | tf_op jit(solution)/shard_map/jit(cholesky)/cholesky | solution.py:59
  192.6 12.1 %cholesky.217 = f32[128,128]{1,0:T(8,128)S(1)} custom-call(f32[128,128]{1,0:T(8,128)S(1)} %cholesky.270), custom_call_target="Cholesky" | custom-call | tf_op jit(solution)/shard_map/jit(cholesky)/cholesky | solution.py:59
  204.7 9.8 %custom-call.32 = f32[1,128,128]{1,2,0:T(8,128)S(1)} custom-call(f32[1,128,128]{2,1,0:T(8,128)S(1)} %get-tuple-element.27), custom_call_target="InvertDiagBlocksLowerTriangular" | custom-call | tf_op jit(solution)/shard_map/jit(cholesky)/cholesky | solution.py:59
  216.1 11.7 %cholesky.238 = f32[128,128]{1,0:T(8,128)S(1)} custom-call(f32[128,128]{1,0:T(8,128)S(1)} %cholesky.275), custom_call_target="Cholesky" | custom-call | tf_op jit(solution)/shard_map/jit(cholesky)/cholesky | solution.py:59
  228.6 9.8 %custom-call.33 = f32[1,128,128]{1,2,0:T(8,128)S(1)} custom-call(f32[1,128,128]{2,1,0:T(8,128)S(1)} %get-tuple-element.24), custom_call_target="InvertDiagBlocksLowerTriangular" | custom-call | tf_op jit(solution)/shard_map/jit(cholesky)/cholesky | solution.py:59
  239.9 11.9 %cholesky.255 = f32[128,128]{1,0:T(8,128)S(1)} custom-call(f32[128,128]{1,0:T(8,128)S(1)} %convolution_subtract_fusion.5), custom_call_target="Cholesky" | custom-call | tf_op jit(solution)/shard_map/jit(cholesky)/cholesky | solution.py:59
  256.7 14.2 %while.1 = (s32[]{:T(128)}, f32[512,512]{1,0:T(8,128)}, s32[4,2]{0,1:T(2,128)S(1)}, f32[4,128,128]{2,1,0:T(8,128)}, s32[]{:T(128)}) while((s32[]{:T(128)}, f32[512,512]{1,0:T(8,128)}, s32[4,2]{0,1:T(2,128)S(1)}, f32[4,128,128]{2,1,0:T(8,128)}, s32[]{:T(128)}) %tuple.31), condition=%wide.while_cond, body=%wide.while_body.sunk | while | flops 2 | bytes 132205 | solution.py:60
  260.9 2.9 bitcast_dynamic-update-slice_fusion.2
  270.9 40.1 %custom-call.34 = f32[4,128,128]{1,2,0:T(8,128)S(1)} custom-call(f32[4,128,128]{2,1,0:T(8,128)} %get-tuple-element.10), custom_call_target="InvertDiagBlocksLowerTriangular" | custom-call | tf_op jit(solution)/shard_map/jit(_solve_triangular)/triangular_solve | solution.py:60
  321.8 12.5 %fusion = f32[1792,512]{1,0:T(8,128)S(1)} fusion(f32[512,1792]{1,0:T(8,128)S(1)} %copy-done, bf16[512,1792]{1,0:T(8,128)(2,1)S(1)} %copy-done.2, f32[128,512]{1,0:T(8,128)S(1)} %fusion.21, f32[128,512]{1,0:T(8,128)S(1)} %fusion.22, f32[128,512]{1,0:T(8,128)S(1)} %fusion.24, f32[128,512]{1,0:T(8,128)S(1)} %fusion.11), kind=kOutput, calls=%fused_computation.6 | convolution fusion | flops 5639766016 | bytes 10223616 | tf_op jit(solution)/shard_map/dot_general | solution.py:39
  334.3 46.5 %all_to_all.5 = f32[8,224,512]{2,1,0:T(8,128)} all-to-all(f32[8,224,512]{2,1,0:T(8,128)S(1)} %bitcast.56), channel_id=1, replica_groups=mesh['tensor_0'=4,'tensor_1'=2,'fsdp_0'=4,'fsdp_1'=4] {'tensor_0','tenso..., dimensions={0} | all-to-all | bytes 7340032 | tf_op jit(solution)/shard_map/all_to_all | solution.py:30
  380.9 3.3 reduce_sum.28
  385.2 6.9 %psum.36 = f32[512]{0:T(512)S(1)} all-reduce(f32[512]{0:T(512)S(1)} %multiply_reduce_fusion), channel_id=1, replica_groups=mesh['tensor_0'=4,'tensor_1'=2,'fsdp_0'=4,'fsdp_1'=4] {'tensor_0'}, use_global_device_ids=true, to_apply=%region_12.13 | all-reduce | flops 512 | bytes 4096 | tf_op jit(solution)/shard_map/psum | solution.py:35
  392.1 5.2 %psum.37 = f32[512]{0:T(512)S(1)} all-reduce(f32[512]{0:T(512)S(1)} %psum.36), channel_id=1, replica_groups=mesh['tensor_0'=4,'tensor_1'=2,'fsdp_0'=4,'fsdp_1'=4] {'tensor_1'}, use_global_device_ids=true, to_apply=%region_13.14 | all-reduce | flops 512 | bytes 4096 | tf_op jit(solution)/shard_map/psum | solution.py:35
  397.2 9.2 %psum.38 = f32[512]{0:T(512)S(1)} all-reduce(f32[512]{0:T(512)S(1)} %psum.37), channel_id=1, replica_groups=mesh['tensor_0'=4,'tensor_1'=2,'fsdp_0'=4,'fsdp_1'=4] {'fsdp_0'}, use_global_device_ids=true, to_apply=%region_14.15 | all-reduce | flops 512 | bytes 4096 | tf_op jit(solution)/shard_map/psum | solution.py:35
  406.4 8.8 %psum.39 = f32[512]{0:T(512)S(1)} all-reduce(f32[512]{0:T(512)S(1)} %psum.38), channel_id=1, replica_groups=mesh['tensor_0'=4,'tensor_1'=2,'fsdp_0'=4,'fsdp_1'=4] {'fsdp_1'}, use_global_device_ids=true, to_apply=%region_15.16 | all-reduce | flops 512 | bytes 4096 | tf_op jit(solution)/shard_map/psum | solution.py:35
  417.9 13.7 %convolution_multiply_fusion = f32[512,1792]{1,0:T(8,128)} fusion(f32[1792,512]{1,0:T(8,128)S(1)} %broadcast_divide_fusion, f32[128,512]{1,0:T(8,128)S(1)} %fusion.21, f32[128,512]{1,0:T(8,128)S(1)} %copy-done.7, f32[128,512]{1,0:T(8,128)S(1)} %fusion.24, f32[128,512]{1,0:T(8,128)S(1)} %fusion.11), kind=kOutput, calls=%fused_computation.4 | convolution fusion | flops 5638848512 | bytes 8388608 | tf_op jit(solution)/shard_map/dot_general | solution.py:49
  431.6 13.7 %multiply_subtract_fusion = f32[512,1792]{1,0:T(8,128)} fusion(f32[1792,512]{1,0:T(8,128)S(1)} %copy-done.4, f32[512,1792]{1,0:T(8,128)S(1)} %copy-done.1, bf16[512,1792]{1,0:T(8,128)(2,1)S(1)} %copy-done.2, f32[128,512]{1,0:T(8,128)S(1)} %fusion.21, f32[128,512]{1,0:T(8,128)S(1)} %copy-done.7, f32[128,512]{1,0:T(8,128)S(1)} %fusion.24, ...), kind=kOutput, calls=%fused_computation.2 | convolution fusion | flops 5641601024 | bytes 13893632 | tf_op jit(solution)/shard_map/dot_general | solution.py:49
  (71 shorter events, 36.4 us)
Async XLA Ops:
  7.2 99.4 %all-reduce.3.cloned.1.call-start = ((), (), s32[]{:S(2)}) async-start(), calls=%async_computation.1 | async-start | bytes 2097152 | tf_op jit(solution)/shard_map/psum | solution.py:68
  17.6 144.8 %all-gather.6.cloned.1.call-start = ((), (), s32[]{:S(2)}) async-start(), calls=%async_computation.3 | async-start | bytes 9437184 | tf_op jit(solution)/shard_map/all_gather | solution.py:18
  111.1 304.2 %all-gather.4.cloned.1.call-start = ((), (), s32[]{:S(2)}) async-start(), calls=%async_computation.2 | async-start | bytes 4128768 | tf_op jit(solution)/shard_map/all_gather | solution.py:74
  167.4 1.0 copy-start.8
  180.1 130.9 %copy-start.5 = (f32[512,512]{1,0:T(8,128)S(1)}, f32[512,512]{1,0:T(8,128)}, u32[]{:S(2)}) copy-start(f32[512,512]{1,0:T(8,128)} %all-reduce.3.cloned.1.call-done) | copy-start | bytes 3145732
  256.7 65.1 %copy-start.2 = (bf16[512,1792]{1,0:T(8,128)(2,1)S(1)}, bf16[512,1792]{1,0:T(8,128)(2,1)}, u32[]{:S(2)}) copy-start(bf16[512,1792]{1,0:T(8,128)(2,1)} %param.4) | copy-start | bytes 5505028
  311.0 0.7 copy-start.9
  311.0 10.8 %copy-start = (f32[512,1792]{1,0:T(8,128)S(1)}, f32[512,1792]{1,0:T(8,128)}, u32[]{:S(2)}) copy-start(f32[512,1792]{1,0:T(8,128)} %param.3) | copy-start | bytes 11010052
  318.0 16.3 %copy-start.6 = (f32[128,512]{1,0:T(8,128)}, f32[128,512]{1,0:T(8,128)S(1)}, u32[]{:S(2)}) copy-start(f32[128,512]{1,0:T(8,128)S(1)} %fusion.22) | copy-start | bytes 786436
  415.3 2.6 copy-start.7
  417.9 13.7 %copy-start.3 = (f32[1792,512]{1,0:T(8,128)}, f32[1792,512]{1,0:T(8,128)S(1)}, u32[]{:S(2)}) copy-start(f32[1792,512]{1,0:T(8,128)S(1)} %broadcast_divide_fusion) | copy-start | bytes 11010052
  417.9 13.7 %copy-start.1 = (f32[512,1792]{1,0:T(8,128)S(1)}, f32[512,1792]{1,0:T(8,128)}, u32[]{:S(2)}) copy-start(f32[512,1792]{1,0:T(8,128)} %param.3) | copy-start | bytes 11010052
  417.9 13.7 %copy-start.4 = (f32[1792,512]{1,0:T(8,128)S(1)}, f32[1792,512]{1,0:T(8,128)}, u32[]{:S(2)}) copy-start(f32[1792,512]{1,0:T(8,128)} %all-gather.4.cloned.1.call-done) | copy-start | bytes 11010052
Sparse Core Ops, SparseCore 0:
  17.7 88.8 all-reduce.2
  111.2 51.0 all-gather.5
  384.3 30.1 all-gather.3
where the time goes:
time: 459 us; the launch traced here: 452 us
  waiting for transfers between devices  140 us (31%)
  other arithmetic  132 us (29%)
  blocking collectives  76.6 us (17%)
  matrix products  70.7 us (15%)
  between operations  16.8 us (4%)
  local copies, waits for them, and re-layouts  15.9 us (3%)
    psum x1, waiting for transfers between devices, per_device(): left = lax.psum(partial_value, FSDP)  88.9 us
    another operation x14, other arithmetic, orthonormal(): lower = jnp.linalg.cholesky(gram)  79 us
    all_gather x1, waiting for transfers between devices, total_of_pieces(): parts = lax.all_gather(value, axis)  51 us
    all_to_all x1, blocking collectives, sum_at_owner(): lax.all_to_all(in_blocks(value, dim, devices), axis, 0, 0, tiled=True)  46.5 us
    another operation x3, other arithmetic, orthonormal(): return jax.scipy.linalg.solve_triangular(lower, block.T, lower=True).T  41.2 us
    psum x4, blocking collectives, over_axes(): return functools.reduce(lax.psum, axes, value)  30.1 us
    dot_general x2, matrix products, outer_rank(): lax.dot_general(first, second, (((1,), (1,)), ((), ())), precision=lax.Pr...  27.3 us
    dot_general x2, matrix products, inner_rows(): lax.dot_general(first, second, (((0,), (0,)), ((), ())), precision=lax.Pr...  17 us
  transfers between devices with their start and end apart: 3, of which 2 were waited for; matrix products, arithmetic and copies ran while one was open for 0% of the time, Pallas kernels for 0%

commit v1 on v0

v1 whole, which is shorter than its diff:
```python
import functools

import jax
import jax.numpy as jnp
from jax import lax
from jax.experimental import pallas as pl
from jax.experimental.pallas import tpu as pltpu
from jax.sharding import Mesh
from jax.sharding import PartitionSpec as P

ROWS = 4096
COLS = 28672
RANK = 512
FSDP = ("fsdp_0", "fsdp_1")
TENSOR = ("tensor_0", "tensor_1")
R = 512
N = 1792
B = 32
MESH = pl.DeviceIdType.MESH
HIGHEST = lax.Precision.HIGHEST
F32 = jnp.float32
BF16 = jnp.bfloat16


def mul(a, b, dims=((1,), (0,)), precision=None):
    return lax.dot_general(a, b, (dims, ((), ())), precision=precision, preferred_element_type=F32)


def halves(x):
    high = x.astype(BF16)
    return high, (x - high.astype(F32)).astype(BF16)


def mul3(ah, al, bh, bl, dims=((1,), (0,))):
    return mul(ah, bh, dims) + (mul(ah, bl, dims) + mul(al, bh, dims))


def factor(block, off):
    n = B // 8
    row = lax.broadcasted_iota(jnp.int32, (8, 128), 0)
    lane = lax.broadcasted_iota(jnp.int32, (8, 128), 1)
    spread = functools.partial(jnp.broadcast_to, shape=(8, 128))
    col = [[None if h < m // 8 else spread(block[8 * h : 8 * h + 8, off + m : off + m + 1]) for h in range(n)] for m in range(B)]
    inv = [(row + 8 * h == lane).astype(F32) for h in range(n)]
    for j in range(B):
        g, s = j // 8, j % 8
        r = lax.rsqrt(spread(col[j][g][s : s + 1, :]))
        low = [None if h < g else col[j][h] * r for h in range(n)]
        top = spread(inv[g][s : s + 1, :]) * r
        inv[g] = jnp.where(row == s, top, inv[g])
        if s < 7:
            inv[g] = inv[g] - jnp.where(row > s, low[g], 0.0) * top
        for h in range(g + 1, n):
            inv[h] = inv[h] - low[h] * top
        for m in range(j + 1, B):
            u = spread(low[m // 8][m % 8 : m % 8 + 1, :])
            for h in range(m // 8, n):
                col[m][h] = col[m][h] - low[h] * u
    return jnp.concatenate(inv, axis=0)


def cholesky_step(aug, k):
    r0 = k * B
    r1 = r0 + B
    lo = 128 * (r0 // 128)
    hi = R + lo + 128
    t = factor(aug[r0:r1, lo : lo + 128], r0 - lo)[:, :B]
    u = mul(t, aug[r0:r1, lo:hi], precision=HIGHEST)
    aug[r0:r1, R:hi] = u[:, R - lo :]
    over_rows = ((0,), (0,))
    if r1 < R:
        r2 = r1 + B
        aug[r1:r2, lo:hi] = aug[r1:r2, lo:hi] - mul(u[:, r1 - lo : r2 - lo], u, over_rows, HIGHEST)
        if r2 < R:
            aug[r2:, lo:hi] = aug[r2:, lo:hi] - mul(u[:, r2 - lo : R - lo], u, over_rows, HIGHEST)


def work(
    mom_ref, grad_ref, rf_ref,
    rt_out, om_ref, odh_ref, odl_ref, d_ref,
    mom, grad, rf, bh, bl, rh, rl, lp, left, rsb, ltf, lth, ltl,
    wp, wo, wr, z1, z2, wf, gsend, grecv, gz, gg, aug, rt, csb,
    in_sem, out_sem,
    ls_send, ls_recv, la_send, la_recv,
    g_send, g_recv, ga_send, ga_recv, gc_send, gc_recv,
    wc_send, wc_recv, wz_send, wz_recv, wd_send, wd_recv,
    cs_send, cs_recv,
):
    z, c = lax.axis_index("tensor_0"), lax.axis_index("tensor_1")
    x, y = lax.axis_index("fsdp_0"), lax.axis_index("fsdp_1")
    other_core = {"tensor_1": 1 - c}

    def one(i):
        return i + 1 - 2 * lax.rem(i, 2), lax.rem(lax.rem(i, 2) + lax.div(i, 2), 2)

    def two(i):
        return 3 - i, lax.div(i, 2)

    (xa, xab), (xb, xbb) = one(x), two(x)
    (ya, yab), (yb, ybb) = one(y), two(y)
    (za, zab), (zb, zbb) = one(z), two(z)
    plane = [({"fsdp_0": xa}, xab), ({"fsdp_1": ya}, yab), ({"fsdp_0": xb}, xbb), ({"fsdp_1": yb}, ybb)]
    orders = [plane[p:] + plane[:p] for p in range(4)]
    column = [({"tensor_0": za}, zab), ({"tensor_0": zb}, zbb)]
    zorders = [[column[q % 2], column[1 - q % 2]] for q in range(4)]

    def rows(start, size):
        return pl.ds(pl.multiple_of(start, 8), size)

    def send(src, dst, send_sem, recv_sem, to):
        copy = pltpu.make_async_remote_copy(src, dst, send_sem, recv_sem, device_id=to, device_id_type=MESH)
        copy.start()
        sent.append(copy)
        return copy

    sent = []

    barrier = pltpu.get_barrier_semaphore()
    plane_peers = [(lax.rem(x + dx, 4), lax.rem(y + dy, 4)) for dx in range(4) for dy in range(4) if dx or dy]
    z_peers = [lax.rem(z + dz, 4) for dz in range(1, 4)]
    for px, py in plane_peers:
        pl.semaphore_signal(barrier, inc=1, device_id={"fsdp_0": px, "fsdp_1": py}, device_id_type=MESH)
    for pz in z_peers:
        pl.semaphore_signal(barrier, inc=1, device_id={"tensor_0": pz}, device_id_type=MESH)
    pl.semaphore_signal(barrier, inc=1, device_id=other_core, device_id_type=MESH)

    ins = []
    for i in range(4):
        s = slice(448 * i, 448 * i + 448)
        ins.append(pltpu.make_async_copy(rf_ref.at[s], rf.at[s], in_sem.at[i]))
    for i in range(2):
        s = slice(256 * i, 256 * i + 256)
        ins.append(pltpu.make_async_copy(mom_ref.at[s], mom.at[s], in_sem.at[4 + i]))
        ins.append(pltpu.make_async_copy(grad_ref.at[s], grad.at[s], in_sem.at[6 + i]))
    for copy in ins:
        copy.start()
    for i in range(4):
        s = slice(448 * i, 448 * i + 448)
        ins[i].wait()
        rh[s, :], rl[s, :] = halves(rf[s, :])

    off = [[128 * p] for p in range(4)]
    for p in range(4):
        for s in range(4):
            off[p].append(off[p][s] + orders[p][s][1] * (64 >> s))
    start_row = [0, 64, 96, 112]
    scatter = [[None] * 4 for _ in range(4)]

    def scatter_send(p, s):
        to, bit = orders[p][s]
        size = 64 >> s
        src = lp.at[rows(off[p][s] + (1 - bit) * size, size)]
        dst = rsb.at[p, start_row[s] : start_row[s] + size]
        scatter[p][s] = send(src, dst, ls_send.at[p, s], ls_recv.at[p, s], to)

    for i in range(2):
        s = slice(256 * i, 256 * i + 256)
        ins[4 + 2 * i].wait()
        ins[5 + 2 * i].wait()
        bh[s, :], bl[s, :] = halves(mom[s, :] + grad[s, :].astype(F32))
        lp[s, :] = mul3(bh[s, :], bl[s, :], rh[...], rl[...])
        if i == 0:
            pl.semaphore_wait(barrier, 19)
        for p in (2 * i, 2 * i + 1):
            scatter_send(p, 0)
    gather = [[None] * 4 for _ in range(4)]

    def gather_send(p, s):
        to, _ = orders[p][s]
        part = left.at[rows(off[p][s + 1], 64 >> s)]
        gather[p][s] = send(part, part, la_send.at[p, s], la_recv.at[p, s], to)

    for s in range(4):
        size = 64 >> s
        for p in range(4):
            scatter[p][s].wait_recv()
            keep = rows(off[p][s + 1], size)
            total = lp[keep, :] + rsb[p, start_row[s] : start_row[s] + size, :]
            if s < 3:
                lp[keep, :] = total
                scatter_send(p, s + 1)
            else:
                left[keep, :] = total
                gather_send(p, 3)
    for s in (3, 2, 1, 0):
        for p in range(4):
            gather[p][s].wait_recv()
            if s:
                gather_send(p, s - 1)

    ltf[...] = left[...].T
    goff = [[256 * c] for p in range(4)]
    for p in range(4):
        for s in range(4):
            goff[p].append(goff[p][s] + orders[p][s][1] * (128 >> s))
    for p in range(4):
        block = left[:, 128 * p : 128 * p + 128]
        rel = goff[p][4] - 256 * c
        gsend[p] = mul(ltf[rows(rel + 256 * (1 - c), 16), :], block, precision=HIGHEST)
    gram_core = send(gsend, grecv, g_send.at[0], g_recv.at[0], other_core)
    gown = []
    for p in range(4):
        block = left[:, 128 * p : 128 * p + 128]
        gown.append(mul(ltf[rows(goff[p][4], 16), :], block, precision=HIGHEST))
    gram_z = []

    def gram_1():
        gram_core.wait_recv()
        for p in range(4):
            gz[z, p] = gown[p] + grecv[p]
        for i, pz in enumerate(z_peers):
            gram_z.append(send(gz.at[z], gz.at[z], g_send.at[1 + i], g_recv.at[1 + i], {"tensor_0": pz}))

    gram_gather = [[None] * 4 for _ in range(4)]

    def gram_send(p, s):
        to, _ = orders[p][s]
        part = gg.at[p, rows(goff[p][s + 1], 128 >> s)]
        gram_gather[p][s] = send(part, part, ga_send.at[p, s], ga_recv.at[p, s], to)

    def gram_2():
        for copy in gram_z:
            copy.wait_recv()
        for p in range(4):
            gg[p, rows(goff[p][4], 16), :] = (gz[0, p] + gz[1, p]) + (gz[2, p] + gz[3, p])
            gram_send(p, 3)

    def gram_3(s):
        for p in range(4):
            gram_gather[p][s].wait_recv()
            if s:
                gram_send(p, s - 1)
            else:
                part = gg.at[p, rows(256 * c, 256)]
                gram_gather[p][0] = send(part, part, gc_send.at[p], gc_recv.at[p], other_core)

    def gram_4():
        for p in range(4):
            gram_gather[p][0].wait_recv()
            aug[:, 128 * p : 128 * p + 128] = gg[p]
        row = lax.broadcasted_iota(jnp.int32, (R, R), 0)
        aug[:, R:] = (row == lax.broadcasted_iota(jnp.int32, (R, R), 1)).astype(F32)

    lth[...], ltl[...] = halves(ltf[...])
    wcore = [None] * 4
    wscatter = [[None, None] for _ in range(4)]
    wgather = [[None, None, None] for _ in range(4)]

    def w_other(i):
        s = rows(256 * (1 - c) + 128 * i, 128)
        wp[128 * i : 128 * i + 128, :] = mul3(lth[s, :], ltl[s, :], bh[...], bl[...])
        for q in (2 * i, 2 * i + 1):
            part = slice(64 * q, 64 * q + 64)
            wcore[q] = send(wp.at[part], wr.at[part], wc_send.at[q], wc_recv.at[q], other_core)

    def w_own(i):
        s = rows(256 * c + 128 * i, 128)
        wo[128 * i : 128 * i + 128, :] = mul3(lth[s, :], ltl[s, :], bh[...], bl[...])

    woff = []
    for q in range(4):
        o1 = 64 * q + 32 * zorders[q][0][1]
        woff.append((64 * q, o1, o1 + 16 * zorders[q][1][1]))

    def w_send(q, s, buf):
        to, bit = zorders[q][s]
        size = 32 >> s
        src = wo.at[rows(woff[q][s] + (1 - bit) * size, size)]
        wscatter[q][s] = send(src, buf.at[q], wz_send.at[q, s], wz_recv.at[q, s], to)

    def w_1(q):
        wcore[q].wait_recv()
        part = slice(64 * q, 64 * q + 64)
        wo[part, :] = wo[part, :] + wr[part, :]
        w_send(q, 0, z1)

    def w_2(q):
        wscatter[q][0].wait_recv()
        keep = rows(woff[q][1], 32)
        wo[keep, :] = wo[keep, :] + z1[q]
        w_send(q, 1, z2)

    def w_gather(q, i, start, size, to):
        part = wf.at[rows(256 * c + start, size)]
        wgather[q][i] = send(part, part, wd_send.at[q, i], wd_recv.at[q, i], to)

    def w_3(q):
        wscatter[q][1].wait_recv()
        wf[rows(256 * c + woff[q][2], 16), :] = wo[rows(woff[q][2], 16), :] + z2[q]
        w_gather(q, 0, woff[q][2], 16, zorders[q][1][0])

    def w_4(q):
        wgather[q][0].wait_recv()
        w_gather(q, 1, woff[q][1], 32, zorders[q][0][0])

    def w_5(q):
        wgather[q][1].wait_recv()
        w_gather(q, 2, woff[q][0], 64, other_core)

    w_other(0)
    gram_1()
    w_other(1)
    gram_2()
    w_own(0)
    gram_3(3)
    w_1(0)
    w_1(1)
    w_own(1)
    gram_3(2)
    w_1(2)
    w_1(3)
    gram_3(1)
    w_2(0)
    w_2(1)
    gram_3(0)
    gram_4()
    between = {
        0: [(w_2, 2), (w_2, 3)],
        2: [(w_3, 0), (w_3, 1)],
        4: [(w_3, 2), (w_3, 3)],
        6: [(w_4, 0), (w_4, 1)],
        8: [(w_4, 2), (w_4, 3)],
        11: [(w_5, 0), (w_5, 1)],
        15: [(w_5, 2), (w_5, 3)],
    }
    for k in range(R // B):
        cholesky_step(aug, k)
        for step, q in between.get(k, []):
            step(q)

    for q in range(4):
        wgather[q][2].wait_recv()
    for i in range(2):
        depth = 256 * i + 256
        ih, il = halves(aug[256 * i : depth, R : R + depth])
        for n in range(0, N, 256):
            wh, wl = halves(wf[:depth, n : n + 256])
            rt[256 * i : depth, n : n + 256] = mul3(ih, il, wh, wl)
    out = pltpu.make_async_copy(rt, rt_out, out_sem)
    out.start()

    me = 4 * x + y
    sums = jnp.zeros((R, 128), F32)
    for n in range(0, N, 128):
        sums = sums + rt[:, n : n + 128] * rt[:, n : n + 128]
    line = [jnp.sum(sums[128 * i : 128 * i + 128].T, axis=0, keepdims=True) for i in range(4)]
    csb[me] = jnp.concatenate(line + [jnp.zeros((4, 128), F32)], axis=0)
    squares = []
    for i, (px, py) in enumerate(plane_peers):
        to = {"fsdp_0": px, "fsdp_1": py}
        squares.append(send(csb.at[me], csb.at[me], cs_send.at[i], cs_recv.at[i], to))
    lh, ll = halves(left[...])
    ih, il = halves(aug[:, R:])
    ortho = mul3(lh, ll, ih, il, ((1,), (1,)))
    om_ref[...] = (ortho * 0.05).astype(BF16)
    for copy in squares:
        copy.wait_recv()
    total = csb[0]
    for i in range(1, 16):
        total = total + csb[i]
    norm = 1.0 / jnp.sqrt(total + 1e-06)
    d = jnp.concatenate([norm[i : i + 1, :] for i in range(4)], axis=1)
    d_ref[...] = jnp.broadcast_to(d, (8, R))
    scale = (ROWS * COLS / RANK) ** 0.5
    odh_ref[...], odl_ref[...] = halves(ortho * (d * scale))
    out.wait()
    for copy in sent:
        copy.wait_send()


def finish(mom, grad, rt, om, odh, odl, d, new_mom, update, new_right):
    right = rt[...]
    rh, rl = halves(right)
    new_mom[...] = mom[...] + grad[...].astype(F32) - mul(om[...], rh)
    update[...] = mul3(odh[...], odl[...], rh, rl)
    new_right[...] = right.T * d[0:1, :]


def per_device(momentum, gradient, right_factor):
    vmem, dma, anywhere = pltpu.VMEM, pltpu.SemaphoreType.DMA, pl.BlockSpec(memory_space=pl.ANY)
    inside = pl.BlockSpec(memory_space=pltpu.VMEM)
    rt, om, odh, odl, d = pl.pallas_call(
        work,
        out_shape=[
            jax.ShapeDtypeStruct((R, N), F32),
            jax.ShapeDtypeStruct((R, RANK), BF16),
            jax.ShapeDtypeStruct((R, RANK), BF16),
            jax.ShapeDtypeStruct((R, RANK), BF16),
            jax.ShapeDtypeStruct((8, RANK), F32),
        ],
        in_specs=[anywhere] * 3,
        out_specs=[anywhere, inside, inside, inside, inside],
        scratch_shapes=[
            vmem((R, N), F32), vmem((R, N), BF16), vmem((N, RANK), F32),
            vmem((R, N), BF16), vmem((R, N), BF16), vmem((N, RANK), BF16), vmem((N, RANK), BF16),
            vmem((R, RANK), F32), vmem((R, RANK), F32), vmem((4, 120, RANK), F32),
            vmem((RANK, R), F32), vmem((RANK, R), BF16), vmem((RANK, R), BF16),
            vmem((256, N), F32), vmem((256, N), F32), vmem((256, N), F32),
            vmem((4, 32, N), F32), vmem((4, 16, N), F32), vmem((RANK, N), F32),
            vmem((4, 16, 128), F32), vmem((4, 16, 128), F32), vmem((4, 4, 16, 128), F32), vmem((4, RANK, 128), F32),
            vmem((RANK, 2 * RANK), F32), vmem((RANK, N), F32), vmem((16, 8, 128), F32),
            dma((8,)), dma,
            dma((4, 4)), dma((4, 4)), dma((4, 4)), dma((4, 4)),
            dma((4,)), dma((4,)), dma((4, 4)), dma((4, 4)), dma((4,)), dma((4,)),
            dma((4,)), dma((4,)), dma((4, 2)), dma((4, 2)), dma((4, 3)), dma((4, 3)),
            dma((15,)), dma((15,)),
        ],
        compiler_params=pltpu.CompilerParams(
            collective_id=0, has_side_effects=True, vmem_limit_bytes=62 << 20
        ),
        name="dion",
    )(momentum, gradient, right_factor)
    wide = 256
    tall = pl.BlockSpec((R, wide), lambda i: (0, i))
    whole = pl.BlockSpec((R, RANK), lambda i: (0, 0))
    return pl.pallas_call(
        finish,
        out_shape=[
            jax.ShapeDtypeStruct((R, N), F32),
            jax.ShapeDtypeStruct((R, N), F32),
            jax.ShapeDtypeStruct((N, RANK), F32),
        ],
        grid=(N // wide,),
        in_specs=[tall, tall, tall, whole, whole, whole, pl.BlockSpec((8, RANK), lambda i: (0, 0))],
        out_specs=[tall, tall, pl.BlockSpec((wide, RANK), lambda i: (i, 0))],
        name="finish",
    )(momentum, gradient, rt, om, odh, odl, d)


def solution(mesh):
    finer = Mesh(mesh.devices.reshape(4, 2, 4, 4), ("tensor_0", "tensor_1", "fsdp_0", "fsdp_1"))
    placed = (P(TENSOR, FSDP), P(TENSOR, FSDP), P(FSDP, None))
    return jax.shard_map(
        per_device,
        mesh=finer,
        in_specs=placed,
        out_specs=(P(TENSOR, FSDP), P(TENSOR, FSDP), P(FSDP, None)),
        check_vma=False,
    )
```

time: 459 us -> 116 us (0.25); the launches traced: 452 us -> 116 us
  waiting for transfers between devices: 140 us -> 0 us
  other arithmetic: 132 us -> 0 us
  Pallas kernels: 0 us -> 115 us
  blocking collectives: 76.6 us -> 0 us
  matrix products: 70.7 us -> 0 us
  between operations: 16.8 us -> 0.64 us
  local copies, waits for them, and re-layouts: 15.9 us -> 0 us
    another operation x17 -> x0, other arithmetic: 120 us -> none  [the longest x14 79 us: orthonormal(): lower = jnp.linalg.cholesky(gram)]
    pallas_call x0 -> x2, Pallas kernels: none -> 115 us  [the longest x1 103 us: per_device(): pl.pallas_call(work, out_shape=[jax.ShapeDtypeStruct((R, N), F32), jax.Sh...]
    psum x1 -> x0, waiting for transfers between devices: 88.9 us -> none  [per_device(): left = lax.psum(partial_value, FSDP)]
    dot_general x5 -> x0, matrix products: 54.7 us -> none  [the longest x2 27.3 us: outer_rank(): lax.dot_general(first, second, (((1,), (1,)), ((), ())), precision=lax.Pr...]
    all_gather x2 -> x0, waiting for transfers between devices: 51 us -> none  [the longest x1 51 us: total_of_pieces(): parts = lax.all_gather(value, axis)]
    all_to_all x1 -> x0, blocking collectives: 46.5 us -> none  [sum_at_owner(): lax.all_to_all(in_blocks(value, dim, devices), axis, 0, 0, tiled=True)]
    psum x4 -> x0, blocking collectives: 30.1 us -> none  [over_axes(): return functools.reduce(lax.psum, axes, value)]
    another operation x13 -> x0, matrix products: 16 us -> none  [the longest x7 10.5 us: orthonormal(): return jax.scipy.linalg.solve_triangular(lower, block.T, lower=True).T]
  transfers between devices with their start and end apart: 3 -> 0, of which waited for: 2 -> 0; matrix products, arithmetic and copies ran while one was open for 0% -> 0% of each run, Pallas kernels for 0% -> 0%
where the time goes in v1:
time: 116 us
  Pallas kernels  115 us (99%)
    pallas_call x1, Pallas kernels, per_device(): pl.pallas_call(work, out_shape=[jax.ShapeDtypeStruct((R, N), F32), jax.Sh...  103 us
    pallas_call x1, Pallas kernels, per_device(): pl.pallas_call(finish, out_shape=[jax.ShapeDtypeStruct((R, N), F32), jax....  12.5 us

profile of v1, /device:TPU:1, one launch (start us, length us, event | category | flops | bytes accessed | tf_op | source)
XLA Modules:
  0.0 116.1 jit_solution(17616199800111466356)
XLA Ops:
  0.6 103.0 %dion.1 = (f32[512,1792]{1,0:T(8,128)}, bf16[512,512]{1,0:T(8,128)(2,1)}, bf16[512,512]{1,0:T(8,128)(2,1)}, bf16[512,512]{1,0:T(8,128)(2,1)}, f32[8,512]{1,0:T(8,128)}) custom-call(f32[512,1792]{1,0:T(8,128)} %mom.1, bf16[512,1792]{1,0:T(8,128)(2,1)} %grad.1, f32[1792,512]{1,0:T(8,128)} %rf_ref.1), custom_call_target="tpu_custom_call" | custom-call | tf_op jit(solution)/shard_map/dion/pallas_call | solution.py:382
  103.6 12.5 %finish.1 = (f32[512,1792]{1,0:T(8,128)}, f32[512,1792]{1,0:T(8,128)}, f32[1792,512]{1,0:T(8,128)}) custom-call(f32[512,1792]{1,0:T(8,128)} %mom.1, bf16[512,1792]{1,0:T(8,128)(2,1)} %grad.1, f32[512,1792]{1,0:T(8,128)} %get-tuple-element.8.rt, bf16[512,512]{1,0:T(8,128)(2,1)} %get-tuple-element.9.om, bf16[512,512]{1,0:T(8,128)(2,1)} %get-tuple-element.10.odh, ...), custom_call_target="tpu_custom_call" | custom-call | tf_op jit(solution)/shard_map/finish/pallas_call | solution.py:416

commit v2 on v1

v2 whole, which is shorter than its diff:
```python
import functools

import jax
import jax.numpy as jnp
from jax import lax
from jax.experimental import pallas as pl
from jax.experimental.pallas import tpu as pltpu
from jax.sharding import Mesh
from jax.sharding import PartitionSpec as P

ROWS = 4096
COLS = 28672
RANK = 512
FSDP = ("fsdp_0", "fsdp_1")
TENSOR = ("tensor_0", "tensor_1")
R = 512
N = 1792
B = 32
MESH = pl.DeviceIdType.MESH
HIGHEST = lax.Precision.HIGHEST
F32 = jnp.float32
BF16 = jnp.bfloat16
NT = ((1,), (1,))


def mul(a, b, dims=((1,), (0,)), precision=None):
    return lax.dot_general(a, b, (dims, ((), ())), precision=precision, preferred_element_type=F32)


def halves(x):
    high = x.astype(BF16)
    return high, (x - high.astype(F32)).astype(BF16)


def mul3(ah, al, bh, bl, dims=((1,), (0,))):
    return mul(ah, bh, dims) + (mul(ah, bl, dims) + mul(al, bh, dims))


def thirds(x):
    high = x.astype(BF16)
    rest = x - high.astype(F32)
    middle = rest.astype(BF16)
    return high, middle, (rest - middle.astype(F32)).astype(BF16)


def spread(x):
    return jnp.broadcast_to(x, (8, 128))


def factor(block, off):
    n = B // 8
    row = lax.broadcasted_iota(jnp.int32, (8, 128), 0)
    lane = lax.broadcasted_iota(jnp.int32, (8, 128), 1) % B
    rest = [block[8 * h : 8 * h + 8] for h in range(n)]
    inv = [(row + 8 * h == lane).astype(F32) for h in range(n)]
    for base in range(0, B, 16):
        end = base + 16
        col = {m: {h: spread(rest[h][:, off + m : off + m + 1]) for h in range(m // 8, n)} for m in range(base, end)}
        for j in range(base, end):
            g, s = j // 8, j % 8
            r = lax.rsqrt(spread(col[j][g][s : s + 1, :]))
            low = {h: col[j][h] * r for h in range(g, n)}
            top = spread(inv[g][s : s + 1, :]) * r
            inv[g] = jnp.where(row == s, top, inv[g])
            if s < 7:
                inv[g] = inv[g] - jnp.where(row > s, low[g], 0.0) * top
            for h in range(g + 1, n):
                inv[h] = inv[h] - low[h] * top
            for m in range(j + 1, end):
                u = spread(low[m // 8][m % 8 : m % 8 + 1, :])
                for h in range(m // 8, n):
                    col[m][h] = col[m][h] - low[h] * u
            if end < B:
                line = spread(rest[g][s : s + 1, :]) * r
                for h in range(g, n):
                    rest[h] = rest[h] - low[h] * line
    return jnp.concatenate(inv, axis=0)


def paired(x):
    high, middle, low = (part.astype(F32) for part in thirds(x))
    place = lax.broadcasted_iota(jnp.int32, x.shape, 1) // B
    first = jnp.where(place % 2 == 0, high, middle).astype(BF16)
    return first, jnp.where(place == 0, low, high).astype(BF16)[:, : 2 * B]


def stacked(x):
    high, middle, low = thirds(x)
    return jnp.concatenate([high, high, middle, middle], axis=0), jnp.concatenate([high, low], axis=0)


def six(first, second):
    return mul(first[0], second[0]) + mul(first[1], second[1])


def cholesky_step(aug, k):
    r0 = k * B
    r1 = r0 + B
    lo = 128 * (r0 // 128)
    hi = R + lo + 128
    off = r0 - lo
    t = factor(aug[r0:r1, lo : lo + 128], off)
    u = six(paired(t), stacked(aug[r0:r1, lo:hi]))
    aug[r0:r1, R:hi] = u[:, R - lo :]
    if r1 == R:
        return
    high, middle, low = thirds(u)
    over = jnp.concatenate([high, middle, high, middle, low, high], axis=0)
    under = jnp.concatenate([high, high, middle, middle, high, low], axis=0)
    top = r1
    while top < R:
        left = 128 * (top // 128)
        end = r1 + B if top == r1 else left + 128
        if end > top:
            part = mul(over[:, top - lo : end - lo], under[:, left - lo :], ((0,), (0,)))
            aug[top:end, left:hi] = aug[top:end, left:hi] - part
        top = end


def work(
    mom_ref, grad_ref, rf_ref,
    rt_out, om_ref, odh_ref, odl_ref, d_ref,
    mom, grad, rf, bh, bl, rh, rl, lp, left, rsb, ltf, lth, ltl,
    wp, wo, wr, z1, z2, wf, gs, gz, gq, aug, rt, csb,
    in_sem, out_sem,
    ls_send, ls_recv, la_send, la_recv,
    g_send, g_recv, ga_send, ga_recv, gc_send, gc_recv,
    wc_send, wc_recv, wz_send, wz_recv, wd_send, wd_recv,
    cs_send, cs_recv,
):
    z, c = lax.axis_index("tensor_0"), lax.axis_index("tensor_1")
    x, y = lax.axis_index("fsdp_0"), lax.axis_index("fsdp_1")
    me = 4 * x + y
    other_core = {"tensor_1": 1 - c}

    def one(i):
        return i + 1 - 2 * lax.rem(i, 2), lax.rem(lax.rem(i, 2) + lax.div(i, 2), 2)

    def two(i):
        return 3 - i, lax.div(i, 2)

    (xa, xab), (xb, xbb) = one(x), two(x)
    (ya, yab), (yb, ybb) = one(y), two(y)
    (za, zab), (zb, zbb) = one(z), two(z)
    plane = [({"fsdp_0": xa}, xab), ({"fsdp_1": ya}, yab), ({"fsdp_0": xb}, xbb), ({"fsdp_1": yb}, ybb)]
    orders = [plane[p:] + plane[:p] for p in range(4)]
    column = [({"tensor_0": za}, zab), ({"tensor_0": zb}, zbb)]
    zorders = [[column[q % 2], column[1 - q % 2]] for q in range(8)]

    def rows(start, size):
        return pl.ds(pl.multiple_of(start, 8), size)

    def send(src, dst, send_sem, recv_sem, to):
        copy = pltpu.make_async_remote_copy(src, dst, send_sem, recv_sem, device_id=to, device_id_type=MESH)
        copy.start()
        sent.append(copy)
        return copy

    sent = []

    barrier = pltpu.get_barrier_semaphore()
    plane_peers = [
        {"fsdp_0": lax.rem(x + dx, 4), "fsdp_1": lax.rem(y + dy, 4)} for dx in range(4) for dy in range(4) if dx or dy
    ]
    tensor_peers = [
        ({"tensor_0": lax.rem(z + dz, 4), "tensor_1": core}, core)
        for dz in range(4)
        for core in ((c, 1 - c) if dz else (1 - c,))
    ]
    for to in plane_peers + [to for to, _ in tensor_peers]:
        pl.semaphore_signal(barrier, inc=1, device_id=to, device_id_type=MESH)

    cuts = [(0, 512), (512, 1024), (1024, 1536), (1536, N)]
    ins = [[] for _ in range(4)]
    for i, (start, end) in enumerate(cuts):
        s = slice(start, end)
        ins[i].append(pltpu.make_async_copy(rf_ref.at[s], rf.at[s], in_sem.at[3 * i]))
        ins[i].append(pltpu.make_async_copy(mom_ref.at[:, s], mom.at[:, s], in_sem.at[3 * i + 1]))
        ins[i].append(pltpu.make_async_copy(grad_ref.at[:, s], grad.at[:, s], in_sem.at[3 * i + 2]))
    for piece in ins:
        for copy in piece:
            copy.start()

    scatter, gather = {}, {}
    flips = [(1, 0), (0, 1), (1, 1)]

    def quarter(p, stage):
        (to0, bit0), (to1, bit1) = orders[p][2 * stage : 2 * stage + 2]
        peers = []
        for f0, f1 in flips:
            to = {**(to0 if f0 else {}), **(to1 if f1 else {})}
            peers.append((to, 2 * (1 - bit0 if f0 else bit0) + (1 - bit1 if f1 else bit1)))
        return 2 * bit0 + bit1, peers

    quarters = [[quarter(p, stage) for stage in range(2)] for p in range(4)]
    large = [128 * p + 32 * quarters[p][0][0] for p in range(4)]
    small = [large[p] + 8 * quarters[p][1][0] for p in range(4)]

    def scatter_send(h, p, stage):
        base, size, place = (128 * p, 32, 0) if stage == 0 else (large[p], 8, 96)
        for i, (to, index) in enumerate(quarters[p][stage][1]):
            k = 3 * stage + i
            dst = rsb.at[h, p, place + size * i : place + size * i + size]
            src = lp.at[h, rows(base + size * index, size)]
            scatter[h, p, k] = send(src, dst, ls_send.at[h, p, k], ls_recv.at[h, p, k], to)

    def gather_send(h, p, stage):
        part = left.at[h, rows(small[p], 8) if stage else rows(large[p], 32)]
        for i, (to, _) in enumerate(quarters[p][stage][1]):
            k = 3 * stage + i
            gather[h, p, k] = send(part, part, la_send.at[h, p, k], la_recv.at[h, p, k], to)

    def left_step(h, i):
        for p in range(4):
            stage = i if i < 2 else 3 - i
            copies = gather if i >= 2 else scatter
            for k in range(3 * stage, 3 * stage + 3):
                copies[h, p, k].wait_recv()
            if i == 0:
                keep = rows(large[p], 32)
                lp[h, keep, :] = (lp[h, keep, :] + rsb[h, p, :32, :]) + (rsb[h, p, 32:64, :] + rsb[h, p, 64:96, :])
                scatter_send(h, p, 1)
            elif i == 1:
                keep = rows(small[p], 8)
                left[h, keep, :] = (lp[h, keep, :] + rsb[h, p, 96:104, :]) + (rsb[h, p, 104:112, :] + rsb[h, p, 112:, :])
                gather_send(h, p, 1)
            elif i == 2:
                gather_send(h, p, 0)

    for i, (start, end) in enumerate(cuts):
        for copy in ins[i]:
            copy.wait()
        s = slice(start, end)
        rh[s, :], rl[s, :] = halves(rf[s, :])
        bh[:, s], bl[:, s] = halves(mom[:, s] + grad[:, s].astype(F32))
        part = mul3(bh[:, s], bl[:, s], rh[s, :256], rl[s, :256])
        lp[0] = part if i == 0 else lp[0] + part
    pl.semaphore_wait(barrier, 22)
    for p in range(4):
        scatter_send(0, p, 0)
    lp[1] = mul3(bh[...], bl[...], rh[:, 256:], rl[:, 256:])
    for p in range(4):
        scatter_send(1, p, 0)

    places = [[(0, 0), (0, 1), (0, 2), (0, 3), (3, 3)], [(1, 1), (1, 2), (1, 3), (2, 2), (2, 3)]]
    grams = []

    def gram_1():
        mine = jnp.concatenate([ltf[rows(128 * t + 8 * me, 8), :] for t in range(4)], axis=0)
        part = [mul(mine, left[h], precision=HIGHEST) for h in range(2)]
        for core in range(2):
            for i, (t, n) in enumerate(places[core]):
                gs[core, i] = part[n // 2][8 * t : 8 * t + 8, 128 * (n % 2) : 128 * (n % 2) + 128]
        slot = 2 * z + c
        for i, (to, core) in enumerate(tensor_peers):
            grams.append(send(gs.at[core], gz.at[slot], g_send.at[i], g_recv.at[i], to))
        gz[slot] = gs[c]

    gathers = []

    def gram_2():
        for copy in grams:
            copy.wait_recv()
        total = gz[0]
        for i in range(1, 8):
            total = total + gz[i]
        gq[c, me] = total
        for i, to in enumerate(plane_peers):
            part = gq.at[c, me]
            gathers.append(send(part, part, ga_send.at[i], ga_recv.at[i], to))

    def gram_3():
        for copy in gathers:
            copy.wait_recv()
        grams.append(send(gq.at[c], gq.at[c], gc_send, gc_recv, other_core))

    def gram_4():
        grams[-1].wait_recv()
        for core in range(2):
            for i, (t, n) in enumerate(places[core]):
                for j in range(16):
                    aug[128 * t + 8 * j : 128 * t + 8 * j + 8, 128 * n : 128 * n + 128] = gq[core, j, i]
        row = lax.broadcasted_iota(jnp.int32, (R, R), 0)
        aug[:, R:] = (row == lax.broadcasted_iota(jnp.int32, (R, R), 1)).astype(F32)

    wcore, wscatter, wgather = {}, {}, {}

    def turn(h):
        half = slice(256 * h, 256 * h + 256)
        ltf[half, :] = left[h].T
        lth[half, :], ltl[half, :] = halves(ltf[half, :])

    def w_other(h):
        s = rows(256 * h + 128 * (1 - c), 128)
        wp[h] = mul3(lth[s, :], ltl[s, :], bh[...], bl[...])
        for q in range(4):
            part = slice(32 * q, 32 * q + 32)
            k = 4 * h + q
            wcore[k] = send(wp.at[h, part], wr.at[h, part], wc_send.at[k], wc_recv.at[k], other_core)

    def w_own(h):
        s = rows(256 * h + 128 * c, 128)
        wo[h] = mul3(lth[s, :], ltl[s, :], bh[...], bl[...])

    woff = []
    for q in range(8):
        o0 = 32 * (q % 4)
        o1 = o0 + 16 * zorders[q][0][1]
        woff.append((o0, o1, o1 + 8 * zorders[q][1][1]))

    def w_send(q, s, buf):
        to, bit = zorders[q][s]
        size = 16 >> s
        src = wo.at[q // 4, rows(woff[q][s] + (1 - bit) * size, size)]
        wscatter[q, s] = send(src, buf.at[q], wz_send.at[q, s], wz_recv.at[q, s], to)

    def w_1(q):
        wcore[q].wait_recv()
        part = slice(woff[q][0], woff[q][0] + 32)
        wo[q // 4, part, :] = wo[q // 4, part, :] + wr[q // 4, part, :]
        w_send(q, 0, z1)

    def w_2(q):
        wscatter[q, 0].wait_recv()
        keep = rows(woff[q][1], 16)
        wo[q // 4, keep, :] = wo[q // 4, keep, :] + z1[q]
        w_send(q, 1, z2)

    def w_gather(q, i, start, size, to):
        part = wf.at[rows(256 * (q // 4) + 128 * c + start, size)]
        wgather[q, i] = send(part, part, wd_send.at[q, i], wd_recv.at[q, i], to)

    def w_3(q):
        wscatter[q, 1].wait_recv()
        own = rows(256 * (q // 4) + 128 * c + woff[q][2], 8)
        wf[own, :] = wo[q // 4, rows(woff[q][2], 8), :] + z2[q]
        w_gather(q, 0, woff[q][2], 8, zorders[q][1][0])

    def w_4(q):
        wgather[q, 0].wait_recv()
        w_gather(q, 1, woff[q][1], 16, zorders[q][0][0])

    def w_5(q):
        wgather[q, 1].wait_recv()
        w_gather(q, 2, woff[q][0], 32, other_core)

    def pairs(step, *firsts):
        return [(step, q) for first in firsts for q in (first, first + 1)]

    for i in range(3):
        left_step(0, i)
        left_step(1, i)
    left_step(0, 3)
    turn(0)
    w_other(0)
    left_step(1, 3)
    turn(1)
    gram_1()
    w_own(0)
    for step, q in pairs(w_1, 0, 2):
        step(q)
    w_other(1)
    w_own(1)
    for step, q in pairs(w_1, 4, 6):
        step(q)
    gram_2()
    for step, q in pairs(w_2, 0, 2):
        step(q)
    gram_3()
    gram_4()
    for step, q in pairs(w_2, 4, 6):
        step(q)
    between = {
        0: pairs(w_3, 0, 2),
        2: pairs(w_3, 4, 6),
        4: pairs(w_4, 0, 2),
        6: pairs(w_4, 4, 6),
        10: pairs(w_5, 0, 2),
        15: pairs(w_5, 4, 6),
    }
    for k in range(R // B):
        cholesky_step(aug, k)
        for step, q in between.get(k, []):
            step(q)

    for q in range(4):
        wgather[q, 2].wait_recv()
    ih, il = halves(aug[:, R : R + 256])
    for n in range(0, N, 256):
        wh, wl = halves(wf[:256, n : n + 256])
        rt[:, n : n + 256] = mul3(ih, il, wh, wl)
    for q in range(4, 8):
        wgather[q, 2].wait_recv()
    ih, il = halves(aug[256:, R + 256 :])
    for n in range(0, N, 256):
        wh, wl = halves(wf[256:, n : n + 256])
        rt[256:, n : n + 256] = rt[256:, n : n + 256] + mul3(ih, il, wh, wl)
    out = pltpu.make_async_copy(rt, rt_out, out_sem)
    out.start()

    sums = jnp.zeros((R, 128), F32)
    for n in range(0, N, 128):
        sums = sums + rt[:, n : n + 128] * rt[:, n : n + 128]
    line = [jnp.sum(sums[128 * i : 128 * i + 128].T, axis=0, keepdims=True) for i in range(4)]
    csb[me] = jnp.concatenate(line + [jnp.zeros((4, 128), F32)], axis=0)
    squares = []
    for i, to in enumerate(plane_peers):
        squares.append(send(csb.at[me], csb.at[me], cs_send.at[i], cs_recv.at[i], to))
    lh, ll = halves(jnp.concatenate([left[0], left[1]], axis=1))
    ih, il = halves(aug[:, R:])
    ortho = mul3(lh, ll, ih, il, NT)
    om_ref[...] = (ortho * 0.05).astype(BF16)
    for copy in squares:
        copy.wait_recv()
    total = csb[0]
    for i in range(1, 16):
        total = total + csb[i]
    norm = 1.0 / jnp.sqrt(total + 1e-06)
    d = jnp.concatenate([norm[i : i + 1, :] for i in range(4)], axis=1)
    d_ref[...] = jnp.broadcast_to(d, (8, R))
    scale = (ROWS * COLS / RANK) ** 0.5
    odh_ref[...], odl_ref[...] = halves(ortho * (d * scale))
    out.wait()
    for copy in sent:
        copy.wait_send()


def finish(mom, grad, rt, om, odh, odl, d, new_mom, update, new_right):
    right = rt[...]
    rh, rl = halves(right)
    new_mom[...] = mom[...] + grad[...].astype(F32) - mul(om[...], rh)
    update[...] = mul3(odh[...], odl[...], rh, rl)
    new_right[...] = right.T * d[0:1, :]


def per_device(momentum, gradient, right_factor):
    vmem, dma, anywhere = pltpu.VMEM, pltpu.SemaphoreType.DMA, pl.BlockSpec(memory_space=pl.ANY)
    inside = pl.BlockSpec(memory_space=pltpu.VMEM)
    rt, om, odh, odl, d = pl.pallas_call(
        work,
        out_shape=[
            jax.ShapeDtypeStruct((R, N), F32),
            jax.ShapeDtypeStruct((R, RANK), BF16),
            jax.ShapeDtypeStruct((R, RANK), BF16),
            jax.ShapeDtypeStruct((R, RANK), BF16),
            jax.ShapeDtypeStruct((8, RANK), F32),
        ],
        in_specs=[anywhere] * 3,
        out_specs=[anywhere, inside, inside, inside, inside],
        scratch_shapes=[
            vmem((R, N), F32), vmem((R, N), BF16), vmem((N, RANK), F32),
            vmem((R, N), BF16), vmem((R, N), BF16), vmem((N, RANK), BF16), vmem((N, RANK), BF16),
            vmem((2, R, 256), F32), vmem((2, R, 256), F32), vmem((2, 4, 120, 256), F32),
            vmem((RANK, R), F32), vmem((RANK, R), BF16), vmem((RANK, R), BF16),
            vmem((2, 128, N), F32), vmem((2, 128, N), F32), vmem((2, 128, N), F32),
            vmem((8, 16, N), F32), vmem((8, 8, N), F32), vmem((RANK, N), F32),
            vmem((2, 5, 8, 128), F32), vmem((8, 5, 8, 128), F32), vmem((2, 16, 5, 8, 128), F32),
            vmem((RANK, 2 * RANK), F32), vmem((RANK, N), F32), vmem((16, 8, 128), F32),
            dma((12,)), dma,
            dma((2, 4, 6)), dma((2, 4, 6)), dma((2, 4, 6)), dma((2, 4, 6)),
            dma((7,)), dma((7,)), dma((15,)), dma((15,)), dma, dma,
            dma((8,)), dma((8,)), dma((8, 2)), dma((8, 2)), dma((8, 3)), dma((8, 3)),
            dma((15,)), dma((15,)),
        ],
        compiler_params=pltpu.CompilerParams(
            collective_id=0, has_side_effects=True, vmem_limit_bytes=62 << 20
        ),
        name="dion",
    )(momentum, gradient, right_factor)
    wide = 896
    tall = pl.BlockSpec((R, wide), lambda i: (0, i))
    whole = pl.BlockSpec((R, RANK), lambda i: (0, 0))
    return pl.pallas_call(
        finish,
        out_shape=[
            jax.ShapeDtypeStruct((R, N), F32),
            jax.ShapeDtypeStruct((R, N), F32),
            jax.ShapeDtypeStruct((N, RANK), F32),
        ],
        grid=(N // wide,),
        in_specs=[tall, tall, tall, whole, whole, whole, pl.BlockSpec((8, RANK), lambda i: (0, 0))],
        out_specs=[tall, tall, pl.BlockSpec((wide, RANK), lambda i: (i, 0))],
        compiler_params=pltpu.CompilerParams(vmem_limit_bytes=56 << 20),
        name="finish",
    )(momentum, gradient, rt, om, odh, odl, d)


def solution(mesh):
    finer = Mesh(mesh.devices.reshape(4, 2, 4, 4), ("tensor_0", "tensor_1", "fsdp_0", "fsdp_1"))
    placed = (P(TENSOR, FSDP), P(TENSOR, FSDP), P(FSDP, None))
    return jax.shard_map(
        per_device,
        mesh=finer,
        in_specs=placed,
        out_specs=(P(TENSOR, FSDP), P(TENSOR, FSDP), P(FSDP, None)),
        check_vma=False,
    )
```

time: 116 us -> 94 us (0.81)
  Pallas kernels: 115 us -> 93.3 us
    pallas_call x1, Pallas kernels: 103 us -> 83.7 us  [per_device(): pl.pallas_call(work, out_shape=[jax.ShapeDtypeStruct((R, N), F32), jax.Sh...]
    pallas_call x1, Pallas kernels: 12.5 us -> 9.55 us  [per_device(): pl.pallas_call(finish, out_shape=[jax.ShapeDtypeStruct((R, N), F32), jax....]
where the time goes in v2:
time: 94 us; the launch traced here: 93.9 us
  Pallas kernels  93.3 us (99%)
    pallas_call x1, Pallas kernels, per_device(): pl.pallas_call(work, out_shape=[jax.ShapeDtypeStruct((R, N), F32), jax.Sh...  83.7 us
    pallas_call x1, Pallas kernels, per_device(): pl.pallas_call(finish, out_shape=[jax.ShapeDtypeStruct((R, N), F32), jax....  9.55 us

profile of v2, /device:TPU:1, one launch (start us, length us, event | category | flops | bytes accessed | tf_op | source)
XLA Modules:
  0.0 93.9 jit_solution(15862114466447269589)
XLA Ops:
  0.6 83.7 %dion.1 = (f32[512,1792]{1,0:T(8,128)}, bf16[512,512]{1,0:T(8,128)(2,1)}, bf16[512,512]{1,0:T(8,128)(2,1)}, bf16[512,512]{1,0:T(8,128)(2,1)}, f32[8,512]{1,0:T(8,128)}) custom-call(f32[512,1792]{1,0:T(8,128)} %mom.1, bf16[512,1792]{1,0:T(8,128)(2,1)} %grad.1, f32[1792,512]{1,0:T(8,128)} %rf_ref.1), custom_call_target="tpu_custom_call" | custom-call | tf_op jit(solution)/shard_map/dion/pallas_call | solution.py:439
  84.4 9.6 %finish.1 = (f32[512,1792]{1,0:T(8,128)}, f32[512,1792]{1,0:T(8,128)}, f32[1792,512]{1,0:T(8,128)}) custom-call(f32[512,1792]{1,0:T(8,128)} %mom.1, bf16[512,1792]{1,0:T(8,128)(2,1)} %grad.1, f32[512,1792]{1,0:T(8,128)} %get-tuple-element.8.rt, bf16[512,512]{1,0:T(8,128)(2,1)} %get-tuple-element.9.om, bf16[512,512]{1,0:T(8,128)(2,1)} %get-tuple-element.10.odh, ...), custom_call_target="tpu_custom_call" | custom-call | tf_op jit(solution)/shard_map/finish/pallas_call | solution.py:473

commit v3 on v2

--- a/solution.py
+++ b/solution.py
@@ -119,7 +119,7 @@
 
 def work(
     mom_ref, grad_ref, rf_ref,
-    rt_out, om_ref, odh_ref, odl_ref, d_ref,
+    rt_out, mom_out, odh_ref, odl_ref, d_ref,
     mom, grad, rf, bh, bl, rh, rl, lp, left, rsb, ltf, lth, ltl,
     wp, wo, wr, z1, z2, wf, gs, gz, gq, aug, rt, csb,
     in_sem, out_sem,
@@ -231,13 +231,14 @@
         for copy in ins[i]:
             copy.wait()
         s = slice(start, end)
-        rh[s, :], rl[s, :] = halves(rf[s, :])
+        rh[s, :256], rl[s, :256] = halves(rf[s, :256])
         bh[:, s], bl[:, s] = halves(mom[:, s] + grad[:, s].astype(F32))
         part = mul3(bh[:, s], bl[:, s], rh[s, :256], rl[s, :256])
         lp[0] = part if i == 0 else lp[0] + part
     pl.semaphore_wait(barrier, 22)
     for p in range(4):
         scatter_send(0, p, 0)
+    rh[:, 256:], rl[:, 256:] = halves(rf[:, 256:])
     lp[1] = mul3(bh[...], bl[...], rh[:, 256:], rl[:, 256:])
     for p in range(4):
         scatter_send(1, p, 0)
@@ -368,15 +369,15 @@
         step(q)
     gram_3()
     gram_4()
-    for step, q in pairs(w_2, 4, 6):
-        step(q)
     between = {
-        0: pairs(w_3, 0, 2),
-        2: pairs(w_3, 4, 6),
-        4: pairs(w_4, 0, 2),
-        6: pairs(w_4, 4, 6),
-        10: pairs(w_5, 0, 2),
-        15: pairs(w_5, 4, 6),
+        1: pairs(w_2, 4, 6),
+        2: pairs(w_3, 0, 2),
+        4: pairs(w_3, 4, 6),
+        6: pairs(w_4, 0, 2),
+        8: pairs(w_4, 4, 6),
+        12: pairs(w_5, 0),
+        13: pairs(w_5, 2),
+        15: pairs(w_5, 4),
     }
     for k in range(R // B):
         cholesky_step(aug, k)
@@ -385,19 +386,19 @@
 
     for q in range(4):
         wgather[q, 2].wait_recv()
-    ih, il = halves(aug[:, R : R + 256])
     for n in range(0, N, 256):
+        if n == 1024:
+            w_5(6)
+        ih, il = halves(aug[:, R : R + 256])
         wh, wl = halves(wf[:256, n : n + 256])
         rt[:, n : n + 256] = mul3(ih, il, wh, wl)
+    w_5(7)
     for q in range(4, 8):
         wgather[q, 2].wait_recv()
     ih, il = halves(aug[256:, R + 256 :])
     for n in range(0, N, 256):
         wh, wl = halves(wf[256:, n : n + 256])
         rt[256:, n : n + 256] = rt[256:, n : n + 256] + mul3(ih, il, wh, wl)
-    out = pltpu.make_async_copy(rt, rt_out, out_sem)
-    out.start()
-
     sums = jnp.zeros((R, 128), F32)
     for n in range(0, N, 128):
         sums = sums + rt[:, n : n + 128] * rt[:, n : n + 128]
@@ -406,10 +407,19 @@
     squares = []
     for i, to in enumerate(plane_peers):
         squares.append(send(csb.at[me], csb.at[me], cs_send.at[i], cs_recv.at[i], to))
+    outs = [pltpu.make_async_copy(rt, rt_out, out_sem.at[0])]
+    outs[0].start()
     lh, ll = halves(jnp.concatenate([left[0], left[1]], axis=1))
     ih, il = halves(aug[:, R:])
     ortho = mul3(lh, ll, ih, il, NT)
-    om_ref[...] = (ortho * 0.05).astype(BF16)
+    small_ortho = (ortho * 0.05).astype(BF16)
+    for start, end in ((0, 768), (768, N)):
+        s = slice(start, end)
+        for n in range(start, end, 256):
+            m = slice(n, n + 256)
+            mom[:, m] = mom[:, m] + grad[:, m].astype(F32) - mul(small_ortho, rt[:, m].astype(BF16))
+        outs.append(pltpu.make_async_copy(mom.at[:, s], mom_out.at[:, s], out_sem.at[len(outs)]))
+        outs[-1].start()
     for copy in squares:
         copy.wait_recv()
     total = csb[0]
@@ -420,33 +430,34 @@
     d_ref[...] = jnp.broadcast_to(d, (8, R))
     scale = (ROWS * COLS / RANK) ** 0.5
     odh_ref[...], odl_ref[...] = halves(ortho * (d * scale))
-    out.wait()
+    for copy in outs:
+        copy.wait()
     for copy in sent:
         copy.wait_send()
 
 
-def finish(mom, grad, rt, om, odh, odl, d, new_mom, update, new_right):
+def finish(mom, rt, odh, odl, d, new_mom, update, new_right):
     right = rt[...]
     rh, rl = halves(right)
-    new_mom[...] = mom[...] + grad[...].astype(F32) - mul(om[...], rh)
     update[...] = mul3(odh[...], odl[...], rh, rl)
+    new_mom[...] = mom[...]
     new_right[...] = right.T * d[0:1, :]
 
 
 def per_device(momentum, gradient, right_factor):
     vmem, dma, anywhere = pltpu.VMEM, pltpu.SemaphoreType.DMA, pl.BlockSpec(memory_space=pl.ANY)
     inside = pl.BlockSpec(memory_space=pltpu.VMEM)
-    rt, om, odh, odl, d = pl.pallas_call(
+    rt, mom, odh, odl, d = pl.pallas_call(
         work,
         out_shape=[
             jax.ShapeDtypeStruct((R, N), F32),
-            jax.ShapeDtypeStruct((R, RANK), BF16),
+            jax.ShapeDtypeStruct((R, N), F32),
             jax.ShapeDtypeStruct((R, RANK), BF16),
             jax.ShapeDtypeStruct((R, RANK), BF16),
             jax.ShapeDtypeStruct((8, RANK), F32),
         ],
         in_specs=[anywhere] * 3,
-        out_specs=[anywhere, inside, inside, inside, inside],
+        out_specs=[anywhere, anywhere, inside, inside, inside],
         scratch_shapes=[
             vmem((R, N), F32), vmem((R, N), BF16), vmem((N, RANK), F32),
             vmem((R, N), BF16), vmem((R, N), BF16), vmem((N, RANK), BF16), vmem((N, RANK), BF16),
@@ -456,7 +467,7 @@
             vmem((8, 16, N), F32), vmem((8, 8, N), F32), vmem((RANK, N), F32),
             vmem((2, 5, 8, 128), F32), vmem((8, 5, 8, 128), F32), vmem((2, 16, 5, 8, 128), F32),
             vmem((RANK, 2 * RANK), F32), vmem((RANK, N), F32), vmem((16, 8, 128), F32),
-            dma((12,)), dma,
+            dma((12,)), dma((3,)),
             dma((2, 4, 6)), dma((2, 4, 6)), dma((2, 4, 6)), dma((2, 4, 6)),
             dma((7,)), dma((7,)), dma((15,)), dma((15,)), dma, dma,
             dma((8,)), dma((8,)), dma((8, 2)), dma((8, 2)), dma((8, 3)), dma((8, 3)),
@@ -478,11 +489,11 @@
             jax.ShapeDtypeStruct((N, RANK), F32),
         ],
         grid=(N // wide,),
-        in_specs=[tall, tall, tall, whole, whole, whole, pl.BlockSpec((8, RANK), lambda i: (0, 0))],
+        in_specs=[tall, tall, whole, whole, pl.BlockSpec((8, RANK), lambda i: (0, 0))],
         out_specs=[tall, tall, pl.BlockSpec((wide, RANK), lambda i: (i, 0))],
         compiler_params=pltpu.CompilerParams(vmem_limit_bytes=56 << 20),
         name="finish",
-    )(momentum, gradient, rt, om, odh, odl, d)
+    )(mom, rt, odh, odl, d)
 
 
 def solution(mesh):

time: 94 us -> 90.7 us (0.965)
  Pallas kernels: 93.3 us -> 90 us
    pallas_call x1, Pallas kernels: 83.7 us -> 81.5 us  [per_device(): pl.pallas_call(work, out_shape=[jax.ShapeDtypeStruct((R, N), F32), jax.Sh...]
    pallas_call x1, Pallas kernels: 9.55 us -> 8.43 us  [per_device(): pl.pallas_call(finish, out_shape=[jax.ShapeDtypeStruct((R, N), F32), jax....]
where the time goes in v3:
time: 90.7 us; the launch traced here: 90.6 us
  Pallas kernels  90 us (99%)
    pallas_call x1, Pallas kernels, per_device(): pl.pallas_call(work, out_shape=[jax.ShapeDtypeStruct((R, N), F32), jax.Sh...  81.5 us
    pallas_call x1, Pallas kernels, per_device(): pl.pallas_call(finish, out_shape=[jax.ShapeDtypeStruct((R, N), F32), jax....  8.43 us

profile of v3, /device:TPU:1, one launch (start us, length us, event | category | flops | bytes accessed | tf_op | source)
XLA Modules:
  0.0 90.6 jit_solution(16462206581081944639)
XLA Ops:
  0.6 81.5 %dion.1 = (f32[512,1792]{1,0:T(8,128)}, f32[512,1792]{1,0:T(8,128)}, bf16[512,512]{1,0:T(8,128)(2,1)}, bf16[512,512]{1,0:T(8,128)(2,1)}, f32[8,512]{1,0:T(8,128)}) custom-call(f32[512,1792]{1,0:T(8,128)} %mom_ref.1, bf16[512,1792]{1,0:T(8,128)(2,1)} %grad_ref.1, f32[1792,512]{1,0:T(8,128)} %rf_ref.1), custom_call_target="tpu_custom_call" | custom-call | tf_op jit(solution)/shard_map/dion/pallas_call | solution.py:450
  82.2 8.4 %finish.1 = (f32[512,1792]{1,0:T(8,128)}, f32[512,1792]{1,0:T(8,128)}, f32[1792,512]{1,0:T(8,128)}) custom-call(f32[512,1792]{1,0:T(8,128)} %get-tuple-element.8.mom, f32[512,1792]{1,0:T(8,128)} %get-tuple-element.9.rt, bf16[512,512]{1,0:T(8,128)(2,1)} %get-tuple-element.10.odh, bf16[512,512]{1,0:T(8,128)(2,1)} %get-tuple-element.11.odl, ...), custom_call_target="tpu_custom_call" | custom-call | tf_op jit(solution)/shard_map/finish/pallas_call | solution.py:484

commit v4 on v3

--- a/solution.py
+++ b/solution.py
@@ -158,6 +158,11 @@
 
     sent = []
 
+    def drain(count):
+        for copy in sent[:count]:
+            copy.wait_send()
+        del sent[:count]
+
     barrier = pltpu.get_barrier_semaphore()
     plane_peers = [
         {"fsdp_0": lax.rem(x + dx, 4), "fsdp_1": lax.rem(y + dy, 4)} for dx in range(4) for dy in range(4) if dx or dy
@@ -364,6 +369,7 @@
     w_own(1)
     for step, q in pairs(w_1, 4, 6):
         step(q)
+    drain(96)
     gram_2()
     for step, q in pairs(w_2, 0, 2):
         step(q)
@@ -393,16 +399,22 @@
         wh, wl = halves(wf[:256, n : n + 256])
         rt[:, n : n + 256] = mul3(ih, il, wh, wl)
     w_5(7)
+
+    def squared(top):
+        sums = jnp.zeros((256, 128), F32)
+        for n in range(0, N, 128):
+            sums = sums + rt[top : top + 256, n : n + 128] * rt[top : top + 256, n : n + 128]
+        return [jnp.sum(sums[i : i + 128].T, axis=0, keepdims=True) for i in (0, 128)]
+
+    line = squared(0)
     for q in range(4, 8):
         wgather[q, 2].wait_recv()
     ih, il = halves(aug[256:, R + 256 :])
     for n in range(0, N, 256):
         wh, wl = halves(wf[256:, n : n + 256])
         rt[256:, n : n + 256] = rt[256:, n : n + 256] + mul3(ih, il, wh, wl)
-    sums = jnp.zeros((R, 128), F32)
-    for n in range(0, N, 128):
-        sums = sums + rt[:, n : n + 128] * rt[:, n : n + 128]
-    line = [jnp.sum(sums[128 * i : 128 * i + 128].T, axis=0, keepdims=True) for i in range(4)]
+
+    line += squared(256)
     csb[me] = jnp.concatenate(line + [jnp.zeros((4, 128), F32)], axis=0)
     squares = []
     for i, to in enumerate(plane_peers):
@@ -420,6 +432,7 @@
             mom[:, m] = mom[:, m] + grad[:, m].astype(F32) - mul(small_ortho, rt[:, m].astype(BF16))
         outs.append(pltpu.make_async_copy(mom.at[:, s], mom_out.at[:, s], out_sem.at[len(outs)]))
         outs[-1].start()
+    drain(len(sent) - len(squares))
     for copy in squares:
         copy.wait_recv()
     total = csb[0]
@@ -432,8 +445,7 @@
     odh_ref[...], odl_ref[...] = halves(ortho * (d * scale))
     for copy in outs:
         copy.wait()
-    for copy in sent:
-        copy.wait_send()
+    drain(len(sent))
 
 
 def finish(mom, rt, odh, odl, d, new_mom, update, new_right):

time: 90.7 us -> 90.4 us (level)
  no operation moved by 1% of the time
where the time goes in v4:
time: 90.4 us; the launch traced here: 90.3 us
  Pallas kernels  89.7 us (99%)
    pallas_call x1, Pallas kernels, per_device(): pl.pallas_call(work, out_shape=[jax.ShapeDtypeStruct((R, N), F32), jax.Sh...  81.2 us
    pallas_call x1, Pallas kernels, per_device(): pl.pallas_call(finish, out_shape=[jax.ShapeDtypeStruct((R, N), F32), jax....  8.44 us

profile of v4, /device:TPU:1, one launch (start us, length us, event | category | flops | bytes accessed | tf_op | source)
XLA Modules:
  0.0 90.3 jit_solution(1197116704913419077)
XLA Ops:
  0.6 81.2 %dion.1 = (f32[512,1792]{1,0:T(8,128)}, f32[512,1792]{1,0:T(8,128)}, bf16[512,512]{1,0:T(8,128)(2,1)}, bf16[512,512]{1,0:T(8,128)(2,1)}, f32[8,512]{1,0:T(8,128)}) custom-call(f32[512,1792]{1,0:T(8,128)} %mom_ref.1, bf16[512,1792]{1,0:T(8,128)(2,1)} %grad_ref.1, f32[1792,512]{1,0:T(8,128)} %rf_ref.1), custom_call_target="tpu_custom_call" | custom-call | tf_op jit(solution)/shard_map/dion/pallas_call | solution.py:462
  81.8 8.4 %finish.1 = (f32[512,1792]{1,0:T(8,128)}, f32[512,1792]{1,0:T(8,128)}, f32[1792,512]{1,0:T(8,128)}) custom-call(f32[512,1792]{1,0:T(8,128)} %get-tuple-element.8.mom, f32[512,1792]{1,0:T(8,128)} %get-tuple-element.9.rt, bf16[512,512]{1,0:T(8,128)(2,1)} %get-tuple-element.10.odh, bf16[512,512]{1,0:T(8,128)(2,1)} %get-tuple-element.11.odl, ...), custom_call_target="tpu_custom_call" | custom-call | tf_op jit(solution)/shard_map/finish/pallas_call | solution.py:496
